TPU v7x, 256 devices: a whole 4x4x8 slice. The times are simulated.
256 devices in a mesh: dp: 4 (over x), ctx: 64 (over z, y, core).
Axes of the slice: x: 4, y: 4, z: 8, core: 2. Of those that a mesh axis runs over, the one named last changes fastest.
Arguments:
- queries: bfloat16 [2, 32768, 2048], P(None, ('dp', 'ctx')), may hold values from -6 to 6
- keys: bfloat16 [2, 32768, 1024], P(None, ('dp', 'ctx')), may hold values from -6 to 6
- values: bfloat16 [2, 32768, 1024], P(None, ('dp', 'ctx')), may hold values from -6 to 6
- doc_start: int32 [2, 32768], P(None, ('dp', 'ctx')), may hold values from 0 to 16383, as said below
- gain_q: float32 [128], replicated, may hold values from 0.5 to 1.5
- key_norm_gain: float32 [128], replicated, may hold values from 0.5 to 1.5
- cotangent: bfloat16 [2, 32768, 2048], P(None, ('dp', 'ctx')), may hold values from -6 to 6
Outputs:
- attended: bfloat16 [2, 32768, 2048], P(None, ('dp', 'ctx'))
- grad_queries: bfloat16 [2, 32768, 2048], P(None, ('dp', 'ctx'))
- grad_keys: bfloat16 [2, 32768, 1024], P(None, ('dp', 'ctx'))
- value_gradients: bfloat16 [2, 32768, 1024], P(None, ('dp', 'ctx'))
- grad_gain_q: float32 [128], replicated
- grad_gain_k: float32 [128], replicated
Inputs may be any that keep to these rules, and one draw needn't show every extreme that they name: doc_start gives each token the position in its sequence of its document's first token; the documents of a sequence are runs of 1 to 256 tokens, the first starting at 0, and every sequence has one of exactly 256 tokens.
All inputs are finite; a program needn't handle non-finite values.
Results may differ from a plain program's by a relative error of at most 0.012.
Values may be sent and summed in bfloat16 or wider, within the bound.
No kernel may reach another device: no remote copies, remote signals or barrier semaphores. Data moves between devices by JAX's collectives and lax.ppermute only.
A program may use at most 128 MiB of HBM per device.

v0:
```python
from functools import partial
import jax
import jax.numpy as jnp
from jax import lax
from jax.sharding import PartitionSpec as P

REACH = 2
query_factor = 168.0 ** (-0.5)
rotary_base = 1000000.0
norm_epsilon = 1e-06


def from_behind(block, axis, distance):
    devices = range(lax.axis_size(axis))
    route = [(i - distance, i) for i in devices if i - distance in devices]
    return lax.ppermute(block, axis, route)


def rotary_angles(position, head_width):
    exponent = jnp.arange(head_width // 2, dtype=jnp.float32) * (2.0 / head_width)
    frequency = jnp.exp(-exponent * jnp.log(jnp.float32(rotary_base)))
    return position.astype(jnp.float32)[..., None] * frequency


def prepare(tensor, gain, angle, factor):
    inverse = lax.rsqrt(jnp.mean(tensor * tensor, axis=-1, keepdims=True) + norm_epsilon)
    normed = tensor * inverse * gain
    middle = tensor.shape[-1] // 2
    cosine = jnp.cos(angle)[..., None, :]
    sine = jnp.sin(angle)[..., None, :]
    first = normed[..., :middle]
    second = normed[..., middle:]
    return (
        jnp.concatenate([first * cosine - second * sine, second * cosine + first * sine], axis=-1)
        * factor
    )


def slot_positions(slot, rows, group, block):
    ascending = slot * block + rows
    descending = slot * block + block - 1 - rows
    inside = (slot >= 0) & (slot < 2 * group)
    return jnp.where(inside, jnp.where(slot < group, ascending, descending), -1)


def visible(doc_query, query_position, key_position):
    return (doc_query[:, :, None] <= key_position[:, None, :]) & (
        key_position[:, None, :] <= query_position[:, :, None]
    )


def forward_terms(q_rot, key_panel, value_panel, mask):
    scores = jnp.einsum("xihrd,xjhd->xhrij", q_rot, key_panel, preferred_element_type=jnp.float32)
    weights = jnp.where(mask[:, None, None], jnp.exp(scores), 0.0)
    summed = jnp.sum(weights, axis=-1)
    mixed = jnp.einsum(
        "xhrij,xjhd->xihrd",
        weights.astype(jnp.bfloat16),
        value_panel,
        preferred_element_type=jnp.float32,
    )
    return (summed, mixed)


def softmax_grads(q_rot, cotangent_heads, key_panel, value_panel, mask, total, delta):
    scores = jnp.einsum("xihrd,xjhd->xhrij", q_rot, key_panel, preferred_element_type=jnp.float32)
    probs = jnp.where(mask[:, None, None], jnp.exp(scores) / total[..., None], 0.0)
    dprob = jnp.einsum(
        "xihrd,xjhd->xhrij", cotangent_heads, value_panel, preferred_element_type=jnp.float32
    )
    dscore = probs * (dprob - delta[..., None])
    return (probs.astype(jnp.bfloat16), dscore.astype(jnp.bfloat16))


def key_grads(probs, dscore, q_rot, cotangent_heads):
    grad_key = jnp.einsum("xhrij,xihrd->xjhd", dscore, q_rot, preferred_element_type=jnp.float32)
    grad_value = jnp.einsum(
        "xhrij,xihrd->xjhd", probs, cotangent_heads, preferred_element_type=jnp.float32
    )
    return (grad_key, grad_value)


def all_grads(q_rot, cotangent_heads, key_panel, value_panel, mask, total, delta):
    probs, dscore = softmax_grads(
        q_rot, cotangent_heads, key_panel, value_panel, mask, total, delta
    )
    grad_key, grad_value = key_grads(probs, dscore, q_rot, cotangent_heads)
    grad_query = jnp.einsum(
        "xhrij,xjhd->xihrd", dscore, key_panel, preferred_element_type=jnp.float32
    )
    return (grad_query, grad_key, grad_value)


def advance(lower, upper, at_fold):
    moved_lower = from_behind(lower, "ctx", 1)
    moved_upper = from_behind(upper, "ctx", -1)
    return (moved_lower, jnp.where(at_fold, lower, moved_upper))


def retreat_grads(lower, upper, at_fold, at_start):
    moved_lower = from_behind(lower, "ctx", -1)
    moved_upper = from_behind(upper, "ctx", 1)
    return (jnp.where(at_fold, upper, moved_lower), jnp.where(at_start, 0.0, moved_upper))


def shards(queries, keys, values, doc_start, gain_q, key_norm_gain, cotangent):
    group = lax.axis_size("ctx")
    block = queries.shape[1]
    head_width = gain_q.shape[0]
    q_heads = queries.shape[2] // head_width
    kv_heads = keys.shape[2] // head_width
    repeat = q_heads // kv_heads
    group_index = lax.axis_index("ctx")
    at_fold = group_index == group - 1
    at_start = group_index == 0
    rows = jnp.arange(block, dtype=jnp.int32)[None, :]
    own_slot = jnp.stack([group_index, 2 * group - 1 - group_index])[:, None]
    own_position = slot_positions(own_slot, rows, group, block)
    angle = rotary_angles(own_position, head_width)
    q_rotated, q_back = jax.vjp(
        lambda tensor, gain: prepare(tensor, gain, angle, query_factor),
        queries.astype(jnp.float32).reshape(2, block, q_heads, head_width),
        gain_q,
    )
    q_rot = q_rotated.astype(jnp.bfloat16).reshape(2, block, kv_heads, repeat, head_width)
    k_rotated, k_back = jax.vjp(
        lambda tensor, gain: prepare(tensor, gain, angle, 1.0),
        keys.astype(jnp.float32).reshape(2, block, kv_heads, head_width),
        key_norm_gain,
    )
    k_rot = k_rotated.astype(jnp.bfloat16)
    cotangent_heads = cotangent.reshape(2, block, kv_heads, repeat, head_width)
    local_key_panel = jnp.stack([k_rot.reshape(2, block, -1), values], axis=1)
    panels = [local_key_panel]
    lower, upper = (local_key_panel[0], local_key_panel[1])
    for step in range(REACH):
        lower, upper = advance(lower, upper, at_fold)
        panels.append(jnp.stack([lower, upper]))
    masks = [
        visible(doc_start, own_position, slot_positions(own_slot - step, rows, group, block))
        for step in range(REACH + 1)
    ]
    zeros_q = jnp.zeros((2, block, kv_heads, repeat, head_width), jnp.float32)
    summed = jnp.zeros((2, kv_heads, repeat, block), jnp.float32)
    mixed = zeros_q
    key_panels = []
    value_panels = []
    for step in range(REACH + 1):
        key_panel = panels[step][:, 0].reshape(2, block, kv_heads, head_width)
        value_panel = panels[step][:, 1].reshape(2, block, kv_heads, head_width)
        key_panels.append(key_panel)
        value_panels.append(value_panel)
        compute = partial(forward_terms, q_rot, key_panel, value_panel, masks[step])
        if step == 0:
            terms = compute()
        else:
            terms = compute()
        summed = summed + terms[0]
        mixed = mixed + terms[1]
    attended_heads = (mixed / jnp.transpose(summed, (0, 3, 1, 2))[..., None]).astype(jnp.bfloat16)
    delta = jnp.einsum(
        "xihrd,xihrd->xhri", cotangent_heads, attended_heads, preferred_element_type=jnp.float32
    )
    grad_q_heads = zeros_q
    for step in range(REACH, -1, -1):
        compute = partial(
            all_grads,
            q_rot,
            cotangent_heads,
            key_panels[step],
            value_panels[step],
            masks[step],
            summed,
            delta,
        )
        if step == 0:
            terms = compute()
        else:
            terms = compute()
        grad_q_heads = grad_q_heads + terms[0]
        contribution = jnp.stack(
            [terms[1].reshape(2, block, -1), terms[2].reshape(2, block, -1)], axis=1
        )
        if step == REACH:
            carried_lower, carried_upper = (contribution[0], contribution[1])
        else:
            carried_lower, carried_upper = retreat_grads(
                carried_lower, carried_upper, at_fold, at_start
            )
            carried_lower = carried_lower + contribution[0]
            carried_upper = carried_upper + contribution[1]
    key_value_gradient = jnp.stack([carried_lower, carried_upper])
    grad_k_heads = key_value_gradient[:, 0].reshape(2, block, kv_heads, head_width)
    grad_v_flat = key_value_gradient[:, 1]
    grad_queries, grad_gain_q = q_back(grad_q_heads.reshape(2, block, q_heads, head_width))
    grad_keys, grad_gain_k = k_back(grad_k_heads)
    grad_gain_q, grad_gain_k = lax.psum((grad_gain_q, grad_gain_k), ("dp", "ctx"))
    return (
        attended_heads.reshape(2, block, -1),
        grad_queries.reshape(2, block, -1).astype(jnp.bfloat16),
        grad_keys.reshape(2, block, -1).astype(jnp.bfloat16),
        grad_v_flat.astype(jnp.bfloat16),
        grad_gain_q,
        grad_gain_k,
    )


def solution(mesh):
    placed = (
        P(None, ("dp", "ctx"), None),
        P(None, ("dp", "ctx"), None),
        P(None, ("dp", "ctx"), None),
        P(None, ("dp", "ctx")),
        P(),
        P(),
        P(None, ("dp", "ctx"), None),
    )
    return jax.shard_map(
        shards,
        mesh=mesh,
        in_specs=placed,
        out_specs=(
            P(None, ("dp", "ctx"), None),
            P(None, ("dp", "ctx"), None),
            P(None, ("dp", "ctx"), None),
            P(None, ("dp", "ctx"), None),
            P(),
            P(),
        ),
        check_vma=False,
    )
```

profile of v0, /device:TPU:1, one launch (start us, length us, event | category | flops | bytes accessed | tf_op | source)
XLA Modules:
  0.0 234.9 jit_solution(2773730723189249938)
XLA Ops:
  8.4 5.1 %collective-permute-start.1 = (bf16[2,128,1024]{1,2,0:T(8,128)(2,1)}, bf16[2,128,1024]{1,2,0:T(8,128)(2,1)}, u32[]{:S(2)}, u32[]{:S(2)}) collective-permute-start(bf16[2,128,1024]{1,2,0:T(8,128)(2,1)} %fusion.65), channel_id=1, source_target_pairs={{1,0},{2,1},{3,2},{4,3},{5,4},{6,5},{7,6},{8,7},{9,8},{10,9},{11,1... | collective-permute-start | bytes 1572872 | tf_op jit(solution)/shard_map/ppermute | solution.py:16
  17.4 2.0 copy.219
  19.3 1.9 copy.220
  21.5 2.9 %fusion.3 = bf16[2,128,8,2,128]{4,1,3,2,0:T(8,128)(2,1)S(1)} fusion(f32[2,128,8,2,64]{4,1,3,2,0:T(8,128)} %bitcast.308, f32[2,128,8,2,64]{4,1,3,2,0:T(8,128)} %bitcast.307), kind=kLoop, calls=%fused_computation.9 | loop fusion | flops 1572864 | bytes 3145728 | tf_op jit(solution)/shard_map/convert_element_type | solution.py:125
  25.4 2.1 broadcast_select_fusion
  27.5 1.9 collective-permute-start
  29.4 2.4 %fusion.15 = (f32[2,8,2,128]{3,2,1,0:T(2,128)}, f32[2,8,128,128,2]{3,2,4,1,0:T(8,128)}) fusion(pred[2,128,128]{1,2,0:T(8,128)(4,1)S(1)} %get-tuple-element.68, bf16[2,128,8,2,128]{4,1,3,2,0:T(8,128)(2,1)S(1)} %fusion.3, bf16[2,128,8,128]{3,1,2,0:T(8,128)(2,1)S(1)} %copy-done.9), kind=kOutput, calls=%fused_computation.48 | convolution fusion | flops 135262208 | bytes 3719168 | tf_op jit(solution)/shard_map/xihrd,xjhd->xhrij/dot_general | solution.py:53
  31.8 3.2 %collective-permute-start.3 = (bf16[2,128,1024]{1,2,0:T(8,128)(2,1)}, bf16[2,128,1024]{1,2,0:T(8,128)(2,1)}, u32[]{:S(2)}, u32[]{:S(2)}) collective-permute-start(bf16[2,128,1024]{1,2,0:T(8,128)(2,1)} %get-tuple-element.48), channel_id=1, source_target_pairs={{1,0},{2,1},{3,2},{4,3},{5,4},{6,5},{7,6},{8,7},{9,8},{10,9},{11,1... | collective-permute-start | bytes 1572872 | tf_op jit(solution)/shard_map/ppermute | solution.py:16
  35.9 2.6 %reshape.655 = bf16[2,128,8,2,128]{4,3,2,1,0:T(2,128)(2,1)} reshape(bf16[2,128,2048]{2,1,0:T(8,128)(2,1)} %param.13) | data formatting | bytes 2097152 | tf_op jit(solution)/shard_map/reshape | solution.py:132
  38.4 3.7 %copy.247 = bf16[2,128,8,2,128]{1,4,3,2,0:T(8,128)(2,1)} copy(bf16[2,128,8,2,128]{4,3,2,1,0:T(2,128)(2,1)} %reshape.655) | data formatting | bytes 2097152 | tf_op jit(solution)/shard_map/reshape | solution.py:132
  42.1 2.7 %collective-permute-start.2 = (bf16[2,128,1024]{1,2,0:T(8,128)(2,1)}, bf16[2,128,1024]{1,2,0:T(8,128)(2,1)S(1)}, u32[]{:S(2)}, u32[]{:S(2)}) collective-permute-start(bf16[2,128,1024]{1,2,0:T(8,128)(2,1)} %collective-permute-done), channel_id=1, source_target_pairs={{0,1},{1,2},{2,3},{3,4},{4,5},{5,6},{6,7},{7,8},{8,9},{9,10},{10,1... | collective-permute-start | bytes 1572872 | tf_op jit(solution)/shard_map/ppermute | solution.py:16
  48.7 2.3 collective-permute-done.2
  54.2 2.4 %bitcast_convert_fusion = (f32[2,8,2,128,128]{3,4,2,1,0:T(8,128)}, bf16[2,128,8,2,128]{1,4,3,2,0:T(8,128)(2,1)}) fusion(f32[2,128,8,2]{1,3,2,0:T(2,128)S(1)} %bitcast.339, f32[2,8,128,2,128]{4,2,3,1,0:T(8,128)S(1)} %fusion.23, f32[2,8,128,2,128]{4,2,3,1,0:T(8,128)S(1)} %fusion.25, f32[2,8,128,128,2]{3,2,4,1,0:T(8,128)S(1)} %copy-done.29, ...), kind=kOutput, calls=%fused_computation.87 | convolution fusion | flops 137887744 | bytes 10010624 | tf_op jit(solution)/shard_map/xhrij,xjhd->xihrd/dot_general | solution.py:56
  56.6 4.2 %copy.285 = f32[2,8,2,128,128]{4,2,1,3,0:T(2,128)} copy(f32[2,8,2,128,128]{3,4,2,1,0:T(8,128)} %get-tuple-element.90) | data formatting | bytes 4194304
  60.8 5.1 %multiply_reduce_fusion = f32[2,8,2,128]{2,1,3,0:T(8,128)} fusion(f32[2,8,2,128,128]{4,2,1,3,0:T(2,128)} %copy.285, bf16[2,128,8,2,128]{4,3,2,1,0:T(2,128)(2,1)} %reshape.655), kind=kLoop, calls=%fused_computation.40 | loop fusion | flops 1568768 | bytes 3162112
  65.9 2.2 copy.286
  68.1 2.5 %fusion.49 = f32[2,8,128,128,1]{2,3,4,1,0:T(8,128)S(1)} fusion(bf16[2,128,8,2,128]{1,4,3,2,0:T(8,128)(2,1)} %copy.247, f32[2,8,128,128,2]{3,2,4,1,0:T(8,128)} %copy-done.13, f32[2,8,2,128]{3,2,1,0:T(2,128)} %bitcast.340, pred[2,128,128]{1,2,0:T(8,128)(4,1)} %get-tuple-element.69), kind=kOutput, calls=%fused_computation.97 | convolution fusion | flops 135790592 | bytes 4243456 | tf_op jit(solution)/shard_map/xhrij,xihrd->xjhd/dot_general | solution.py:77
  75.7 2.1 collective-permute-start.5
  80.8 11.8 %collective-permute-done.5 = f32[2,128,1024]{1,2,0:T(8,128)S(1)} collective-permute-done((f32[2,128,1024]{1,2,0:T(8,128)S(1)}, f32[2,128,1024]{1,2,0:T(8,128)S(1)}, u32[]{:S(2)}, u32[]{:S(2)}) %collective-permute-start.5) | collective-permute-done | bytes 1048608 | tf_op jit(solution)/shard_map/ppermute | solution.py:16
  94.1 1.9 collective-permute-start.4
  96.0 3.6 %collective-permute-start.6 = (f32[2,128,1024]{1,2,0:T(8,128)}, f32[2,128,1024]{1,2,0:T(8,128)}, u32[]{:S(2)}, u32[]{:S(2)}) collective-permute-start(f32[2,128,1024]{1,2,0:T(8,128)} %get-tuple-element.44), channel_id=1, source_target_pairs={{1,0},{2,1},{3,2},{4,3},{5,4},{6,5},{7,6},{8,7},{9,8},{10,9},{11,1... | collective-permute-start | bytes 3145736 | tf_op jit(solution)/shard_map/ppermute | solution.py:16
  101.1 3.3 %copy.325 = f32[2,128,16,64]{3,2,1,0:T(8,128)} copy(f32[2,128,16,64]{1,3,2,0:T(8,128)} %get-tuple-element.58) | data formatting | bytes 2097152
  104.4 3.3 %copy.326 = f32[2,128,16,64]{3,2,1,0:T(8,128)} copy(f32[2,128,16,64]{1,3,2,0:T(8,128)} %get-tuple-element.59) | data formatting | bytes 2097152
  107.7 1.9 fusion.89
  112.5 3.0 %fusion.32 = (f32[1,2,128,1024]{2,3,1,0:T(8,128)S(1)}, f32[2,128,1024]{1,2,0:T(8,128)}) fusion(f32[2,1,128,1024]{2,3,1,0:T(8,128)S(1)} %bitcast.301, f32[2,1,128,1024]{2,3,1,0:T(8,128)S(1)} %bitcast.319, f32[2,128,1024]{1,2,0:T(8,128)} %collective-permute-done.6, pred[]{:T(512)S(6)} %eq.6, f32[2,1,128,1024]{2,3,1,0:T(8,128)S(1)} %bitcast.323, ...), kind=kLoop, calls=%fused_computation.63 | loop fusion | flops 1572864 | bytes 8388610 | tf_op jit(solution)/shard_map/stack | solution.py:192
  115.5 2.0 collective-permute-start.7
  118.2 2.5 %multiply_reduce_fusion.1 = (f32[128]{0:T(128)}, f32[2,128,16]{2,1,0:T(8,128)}) fusion(f32[2,128,16]{2,1,0:T(8,128)S(1)} %copy.218, f32[2,128,16,64]{3,2,1,0:T(8,128)S(1)} %get-tuple-element.53, f32[2,128,16,64]{3,2,1,0:T(8,128)S(1)} %get-tuple-element.52, f32[128]{0:T(128)S(1)} %copy-done.60, f32[2,128,16,128]{3,2,1,0:T(8,128)S(1)} %bitcast.299), kind=kLoop, calls=%fused_computation.41 | loop fusion | flops 3665792 | bytes 4228096 | tf_op jit(solution)/shard_map/transpose(jvp())/reduce_sum | solution.py:27
  120.7 1.6 copy.242
  125.1 4.8 %fusion = bf16[2,128,16,128]{3,2,1,0:T(8,128)(2,1)} fusion(f32[2,128,16]{2,1,0:T(8,128)} %copy.243, f32[128]{0:T(128)} %param.11, f32[2,128,16]{2,1,0:T(8,128)S(1)} %copy.218, f32[2,128,16,64]{3,2,1,0:T(8,128)} %copy-done.1, f32[2,128,16,64]{3,2,1,0:T(8,128)} %copy-done, f32[2,128,16,128]{3,2,1,0:T(8,128)S(1)} %bitcast.300), kind=kLoop, calls=%fused_computation.1 | loop fusion | flops 3670016 | bytes 5276160 | tf_op jit(solution)/shard_map/convert_element_type | solution.py:200
  129.9 2.4 %convert_element_type.84 = bf16[2,128,2048]{2,1,0:T(8,128)(2,1)} reshape(bf16[2,128,16,128]{3,2,1,0:T(8,128)(2,1)} %fusion) | data formatting | bytes 2097152 | tf_op jit(solution)/shard_map/convert_element_type | solution.py:200
  139.0 1.6 multiply_add_fusion.4
  143.9 91.0 %all-reduce.4 = (f32[128]{0:T(128)}, f32[128]{0:T(128)}) all-reduce(f32[128]{0:T(128)S(1)} %copy-done.72, f32[128]{0:T(128)S(1)} %get-tuple-element.38), channel_id=1, replica_groups=mesh['dp'=4,'ctx'=64] {'dp','ctx'}, use_global_device_ids=true, to_apply=%region_8.9 | all-reduce | flops 256 | bytes 2048 | tf_op jit(solution)/shard_map/psum | solution.py:197
  (216 shorter events, 47.2 us)
Async XLA Ops:
  0.6 4.8 %copy-start.61 = (f32[128]{0:T(128)S(1)}, f32[128]{0:T(128)}, u32[]{:S(2)}) copy-start(f32[128]{0:T(128)} %param.12) | copy-start | bytes 1540
  6.5 7.1 %copy-start.8 = (bf16[2,128,8,128]{3,1,2,0:T(8,128)(2,1)}, bf16[2,128,8,128]{3,1,2,0:T(8,128)(2,1)S(1)}, u32[]{:S(2)}) copy-start(bf16[2,128,8,128]{3,1,2,0:T(8,128)(2,1)S(1)} %maximum_convert_fusion) | copy-start | bytes 1572868
  7.2 6.3 %copy-start.19 = (bf16[2,128,8,128]{1,3,2,0:T(8,128)(2,1)}, bf16[2,128,8,128]{1,3,2,0:T(8,128)(2,1)S(1)}, u32[]{:S(2)}) copy-start(bf16[2,128,8,128]{1,3,2,0:T(8,128)(2,1)S(1)} %copy.223) | copy-start | bytes 1572868
  7.5 6.1 %copy-start.21 = (bf16[2,128,1024]{1,2,0:T(8,128)(2,1)}, bf16[2,128,1024]{1,2,0:T(8,128)(2,1)S(1)}, u32[]{:S(2)}) copy-start(bf16[2,128,1024]{1,2,0:T(8,128)(2,1)S(1)} %copy.224) | copy-start | bytes 1572868
  8.4 17.0 %collective-permute-start.1 = (bf16[2,128,1024]{1,2,0:T(8,128)(2,1)}, bf16[2,128,1024]{1,2,0:T(8,128)(2,1)}, u32[]{:S(2)}, u32[]{:S(2)}) collective-permute-start(bf16[2,128,1024]{1,2,0:T(8,128)(2,1)} %fusion.65), channel_id=1, source_target_pairs={{1,0},{2,1},{3,2},{4,3},{5,4},{6,5},{7,6},{8,7},{9,8},{10,9},{11,1... | collective-permute-start | bytes 1572872 | tf_op jit(solution)/shard_map/ppermute | solution.py:16
  21.4 3.1 %copy-start.63 = (pred[2]{0:T(512)(128)(4,1)S(1)}, pred[2]{0:T(512)(128)(4,1)}, u32[]{:S(2)}) copy-start(pred[2]{0:T(512)(128)(4,1)} %get-tuple-element.78) | copy-start | bytes 10
  21.4 3.1 %copy-start.64 = (pred[2]{0:T(512)(128)(4,1)S(1)}, pred[2]{0:T(512)(128)(4,1)}, u32[]{:S(2)}) copy-start(pred[2]{0:T(512)(128)(4,1)} %get-tuple-element.79) | copy-start | bytes 10
  21.4 3.1 %copy-start.65 = (pred[2]{0:T(512)(128)(4,1)S(1)}, pred[2]{0:T(512)(128)(4,1)}, u32[]{:S(2)}) copy-start(pred[2]{0:T(512)(128)(4,1)} %get-tuple-element.80) | copy-start | bytes 10
  21.4 3.1 %copy-start.66 = (pred[2]{0:T(512)(128)(4,1)S(1)}, pred[2]{0:T(512)(128)(4,1)}, u32[]{:S(2)}) copy-start(pred[2]{0:T(512)(128)(4,1)} %get-tuple-element.81) | copy-start | bytes 10
  21.4 3.1 %copy-start.67 = (s32[2]{0:T(128)S(1)}, s32[2]{0:T(128)}, u32[]{:S(2)}) copy-start(s32[2]{0:T(128)} %get-tuple-element.46) | copy-start | bytes 28
  21.5 3.1 %copy-start.58 = (s32[2,128]{1,0:T(2,128)S(1)}, s32[2,128]{1,0:T(2,128)}, u32[]{:S(2)}) copy-start(s32[2,128]{1,0:T(2,128)} %get-tuple-element.51) | copy-start | bytes 3076
  21.5 3.1 %copy-start.71 = (s32[2,128]{1,0:T(2,128)S(1)}, s32[2,128]{1,0:T(2,128)}, u32[]{:S(2)}) copy-start(s32[2,128]{1,0:T(2,128)} %param.10) | copy-start | bytes 3076
  21.5 3.9 %copy-start.20 = (bf16[2,128,8,128]{1,3,2,0:T(8,128)(2,1)S(1)}, bf16[2,128,8,128]{1,3,2,0:T(8,128)(2,1)}, u32[]{:S(2)}) copy-start(bf16[2,128,8,128]{1,3,2,0:T(8,128)(2,1)} %copy-done.19) | copy-start | bytes 1572868
  21.5 3.9 %copy-start.22 = (bf16[2,128,1024]{1,2,0:T(8,128)(2,1)S(1)}, bf16[2,128,1024]{1,2,0:T(8,128)(2,1)}, u32[]{:S(2)}) copy-start(bf16[2,128,1024]{1,2,0:T(8,128)(2,1)} %copy-done.21) | copy-start | bytes 1572868
  24.4 5.0 %copy-start.9 = (bf16[2,128,8,128]{3,1,2,0:T(8,128)(2,1)S(1)}, bf16[2,128,8,128]{3,1,2,0:T(8,128)(2,1)}, u32[]{:S(2)}) copy-start(bf16[2,128,8,128]{3,1,2,0:T(8,128)(2,1)} %copy-done.8) | copy-start | bytes 1572868
  25.4 6.4 %copy-start.49 = (pred[2,128,128]{1,2,0:T(8,128)(4,1)}, pred[2,128,128]{1,2,0:T(8,128)(4,1)S(1)}, u32[]{:S(2)}) copy-start(pred[2,128,128]{1,2,0:T(8,128)(4,1)S(1)} %get-tuple-element.68) | copy-start | bytes 98308
  27.5 14.6 %collective-permute-start = (bf16[2,128,1024]{1,2,0:T(8,128)(2,1)}, bf16[2,128,1024]{1,2,0:T(8,128)(2,1)}, u32[]{:S(2)}, u32[]{:S(2)}) collective-permute-start(bf16[2,128,1024]{1,2,0:T(8,128)(2,1)} %get-tuple-element.49), channel_id=1, source_target_pairs={{0,1},{1,2},{2,3},{3,4},{4,5},{5,6},{6,7},{7,8},{8,9},{9,10},{10,1... | collective-permute-start | bytes 1572872 | tf_op jit(solution)/shard_map/ppermute | solution.py:16
  31.8 14.9 %collective-permute-start.3 = (bf16[2,128,1024]{1,2,0:T(8,128)(2,1)}, bf16[2,128,1024]{1,2,0:T(8,128)(2,1)}, u32[]{:S(2)}, u32[]{:S(2)}) collective-permute-start(bf16[2,128,1024]{1,2,0:T(8,128)(2,1)} %get-tuple-element.48), channel_id=1, source_target_pairs={{1,0},{2,1},{3,2},{4,3},{5,4},{6,5},{7,6},{8,7},{9,8},{10,9},{11,1... | collective-permute-start | bytes 1572872 | tf_op jit(solution)/shard_map/ppermute | solution.py:16
  42.1 4.0 %copy-start.43 = (pred[2,128,128]{1,2,0:T(8,128)(4,1)S(1)}, pred[2,128,128]{1,2,0:T(8,128)(4,1)}, u32[]{:S(2)}) copy-start(pred[2,128,128]{1,2,0:T(8,128)(4,1)} %get-tuple-element.70) | copy-start | bytes 98308
  42.1 8.9 %collective-permute-start.2 = (bf16[2,128,1024]{1,2,0:T(8,128)(2,1)}, bf16[2,128,1024]{1,2,0:T(8,128)(2,1)S(1)}, u32[]{:S(2)}, u32[]{:S(2)}) collective-permute-start(bf16[2,128,1024]{1,2,0:T(8,128)(2,1)} %collective-permute-done), channel_id=1, source_target_pairs={{0,1},{1,2},{2,3},{3,4},{4,5},{5,6},{6,7},{7,8},{8,9},{9,10},{10,1... | collective-permute-start | bytes 1572872 | tf_op jit(solution)/shard_map/ppermute | solution.py:16
  53.1 3.5 %copy-start.56 = (f32[2,2,8,128]{3,2,1,0:T(8,128)}, f32[2,2,8,128]{3,2,1,0:T(8,128)S(1)}, u32[]{:S(2)}) copy-start(f32[2,2,8,128]{3,2,1,0:T(8,128)S(1)} %add_add_fusion.2) | copy-start | bytes 49156
  75.1 3.1 %copy-start.26 = (bf16[2,8,2,128,128]{3,4,2,1,0:T(8,128)(2,1)}, bf16[2,8,2,128,128]{3,4,2,1,0:T(8,128)(2,1)S(1)}, u32[]{:S(2)}) copy-start(bf16[2,8,2,128,128]{3,4,2,1,0:T(8,128)(2,1)S(1)} %fusion.5) | copy-start | bytes 3145732
  75.7 16.9 %collective-permute-start.5 = (f32[2,128,1024]{1,2,0:T(8,128)S(1)}, f32[2,128,1024]{1,2,0:T(8,128)S(1)}, u32[]{:S(2)}, u32[]{:S(2)}) collective-permute-start(f32[2,128,1024]{1,2,0:T(8,128)S(1)} %fusion.44), channel_id=1, source_target_pairs={{1,0},{2,1},{3,2},{4,3},{5,4},{6,5},{7,6},{8,7},{9,8},{10,9},{11,1... | collective-permute-start | bytes 3145736 | tf_op jit(solution)/shard_map/ppermute | solution.py:16
  79.8 12.9 %copy-start.6 = (f32[2,8,128,128,1]{3,2,4,1,0:T(8,128)}, f32[2,8,128,128,1]{3,2,4,1,0:T(8,128)S(1)}, u32[]{:S(2)}) copy-start(f32[2,8,128,128,1]{3,2,4,1,0:T(8,128)S(1)} %fusion.88) | copy-start | bytes 3145732
  80.8 13.3 %copy-start.27 = (f32[2,8,128,128,1]{2,3,4,1,0:T(8,128)}, f32[2,8,128,128,1]{2,3,4,1,0:T(8,128)S(1)}, u32[]{:S(2)}) copy-start(f32[2,8,128,128,1]{2,3,4,1,0:T(8,128)S(1)} %fusion.47) | copy-start | bytes 3145732
  94.1 17.3 %collective-permute-start.4 = (f32[2,128,1024]{1,2,0:T(8,128)}, f32[2,128,1024]{1,2,0:T(8,128)}, u32[]{:S(2)}, u32[]{:S(2)}) collective-permute-start(f32[2,128,1024]{1,2,0:T(8,128)} %get-tuple-element.45), channel_id=1, source_target_pairs={{0,1},{1,2},{2,3},{3,4},{4,5},{5,6},{6,7},{7,8},{8,9},{9,10},{10,1... | collective-permute-start | bytes 3145736 | tf_op jit(solution)/shard_map/ppermute | solution.py:16
  96.0 16.4 %collective-permute-start.6 = (f32[2,128,1024]{1,2,0:T(8,128)}, f32[2,128,1024]{1,2,0:T(8,128)}, u32[]{:S(2)}, u32[]{:S(2)}) collective-permute-start(f32[2,128,1024]{1,2,0:T(8,128)} %get-tuple-element.44), channel_id=1, source_target_pairs={{1,0},{2,1},{3,2},{4,3},{5,4},{6,5},{7,6},{8,7},{9,8},{10,9},{11,1... | collective-permute-start | bytes 3145736 | tf_op jit(solution)/shard_map/ppermute | solution.py:16
  111.3 4.2 %copy-start.25 = (f32[2,8,128,128,1]{2,3,4,1,0:T(8,128)}, f32[2,8,128,128,1]{2,3,4,1,0:T(8,128)S(1)}, u32[]{:S(2)}) copy-start(f32[2,8,128,128,1]{2,3,4,1,0:T(8,128)S(1)} %fusion.45) | copy-start | bytes 3145732
  112.4 5.1 %copy-start.15 = (f32[2,128,16,64]{3,2,1,0:T(8,128)S(1)}, f32[2,128,16,64]{3,2,1,0:T(8,128)}, u32[]{:S(2)}) copy-start(f32[2,128,16,64]{3,2,1,0:T(8,128)} %copy.325) | copy-start | bytes 3145732
  112.5 5.1 %copy-start.16 = (f32[2,128,16,64]{3,2,1,0:T(8,128)S(1)}, f32[2,128,16,64]{3,2,1,0:T(8,128)}, u32[]{:S(2)}) copy-start(f32[2,128,16,64]{3,2,1,0:T(8,128)} %copy.326) | copy-start | bytes 3145732
  115.5 18.2 %collective-permute-start.7 = (f32[2,128,1024]{1,2,0:T(8,128)}, f32[2,128,1024]{1,2,0:T(8,128)}, u32[]{:S(2)}, u32[]{:S(2)}) collective-permute-start(f32[2,128,1024]{1,2,0:T(8,128)} %get-tuple-element.43), channel_id=1, source_target_pairs={{0,1},{1,2},{2,3},{3,4},{4,5},{5,6},{6,7},{7,8},{8,9},{9,10},{10,1... | collective-permute-start | bytes 3145736 | tf_op jit(solution)/shard_map/ppermute | solution.py:16
  129.9 3.8 %copy-start.5 = (f32[2,8,128,128,1]{3,2,4,1,0:T(8,128)S(1)}, f32[2,8,128,128,1]{3,2,4,1,0:T(8,128)}, u32[]{:S(2)}) copy-start(f32[2,8,128,128,1]{3,2,4,1,0:T(8,128)} %copy-done.4) | copy-start | bytes 3145732
  (49 other events, 103.0 us)
where the time goes:
time: 236 us; the launch traced here: 235 us
  blocking collectives  91 us (39%)
  local copies, waits for them, and re-layouts  45.8 us (19%)
  other arithmetic  40.8 us (17%)
  starting transfers between devices  22.5 us (10%)
  matrix products  17.9 us (8%)
  waiting for transfers between devices  15.2 us (6%)
    psum x1, blocking collectives, shards(): lax.psum((grad_gain_q, grad_gain_k), ('dp', 'ctx'))  91 us
    unnamed x158, local copies, waits for them, and re-layouts  24.7 us
    ppermute x8, starting transfers between devices, from_behind(): return lax.ppermute(block, axis, route)  22.5 us
    ppermute x8, waiting for transfers between devices, from_behind(): return lax.ppermute(block, axis, route)  15.2 us
    reshape x2, local copies, waits for them, and re-layouts, shards(): cotangent_heads = cotangent.reshape(2, block, kv_heads, repeat, head_width)  6.23 us
    unnamed x1, other arithmetic  5.11 us
    convert_element_type x1, other arithmetic, shards(): grad_queries.reshape(2, block, -1).astype(jnp.bfloat16)  4.83 us
  transfers between devices with their start and end apart: 8, of which 3 were waited for; matrix products, arithmetic and copies ran while one was open for 23% of the time, Pallas kernels for 0%

commit v1 on v0

--- a/solution.py
+++ b/solution.py
@@ -3,11 +3,18 @@
 import jax.numpy as jnp
 from jax import lax
 from jax.sharding import PartitionSpec as P
+from jax.lax import psum
 
 REACH = 2
 query_factor = 168.0 ** (-0.5)
 rotary_base = 1000000.0
 norm_epsilon = 1e-06
+
+
+def mark_array_on(block_in, dev_axis, shard_axis):
+    tmp = psum(block_in, axis_name=dev_axis)
+    outer = psum(tmp, axis_name=shard_axis)
+    return outer
 
 
 def from_behind(block, axis, distance):
@@ -194,7 +201,7 @@
     grad_v_flat = key_value_gradient[:, 1]
     grad_queries, grad_gain_q = q_back(grad_q_heads.reshape(2, block, q_heads, head_width))
     grad_keys, grad_gain_k = k_back(grad_k_heads)
-    grad_gain_q, grad_gain_k = lax.psum((grad_gain_q, grad_gain_k), ("dp", "ctx"))
+    grad_gain_q, grad_gain_k = mark_array_on((grad_gain_q, grad_gain_k), "dp", "ctx")
     return (
         attended_heads.reshape(2, block, -1),
         grad_queries.reshape(2, block, -1).astype(jnp.bfloat16),

time: 236 us -> 292 us (1.24)
  the two profiles are of different devices: /device:TPU:1 before, /device:TPU:128 now
where the time goes in v1:
time: 292 us; the launch traced here: 291 us
  blocking collectives  136 us (47%)
  local copies, waits for them, and re-layouts  45.8 us (16%)
  other arithmetic  40.7 us (14%)
  starting transfers between devices  28.3 us (10%)
  waiting for transfers between devices  19.8 us (7%)
  matrix products  17.9 us (6%)
    psum x1, blocking collectives, mark_array_on(): outer = psum(tmp, axis_name=shard_axis)  126 us
    ppermute x8, starting transfers between devices, from_behind(): return lax.ppermute(block, axis, route)  28.3 us
    unnamed x158, local copies, waits for them, and re-layouts  24.7 us
    ppermute x8, waiting for transfers between devices, from_behind(): return lax.ppermute(block, axis, route)  19.8 us
    psum x1, blocking collectives, mark_array_on(): tmp = psum(block_in, axis_name=dev_axis)  10.5 us
    reshape x2, local copies, waits for them, and re-layouts, shards(): cotangent_heads = cotangent.reshape(2, block, kv_heads, repeat, head_width)  6.24 us
  transfers between devices with their start and end apart: 8, of which 4 were waited for; matrix products, arithmetic and copies ran while one was open for 19% of the time, Pallas kernels for 0%

profile of v1, /device:TPU:128, one launch (start us, length us, event | category | flops | bytes accessed | tf_op | source)
XLA Modules:
  0.0 290.6 jit_solution(11939150100067765988)
XLA Ops:
  8.4 3.9 %collective-permute-start.1 = (bf16[2,128,1024]{1,2,0:T(8,128)(2,1)}, bf16[2,128,1024]{1,2,0:T(8,128)(2,1)}, u32[]{:S(2)}, u32[]{:S(2)}) collective-permute-start(bf16[2,128,1024]{1,2,0:T(8,128)(2,1)} %fusion.65), channel_id=1, source_target_pairs={{1,0},{2,1},{3,2},{4,3},{5,4},{6,5},{7,6},{8,7},{9,8},{10,9},{11,1... | collective-permute-start | bytes 1572872 | tf_op jit(solution)/shard_map/ppermute | solution.py:23
  16.1 2.0 copy.219
  18.0 2.0 copy.220
  20.2 2.9 %fusion.3 = bf16[2,128,8,2,128]{4,1,3,2,0:T(8,128)(2,1)S(1)} fusion(f32[2,128,8,2,64]{4,1,3,2,0:T(8,128)} %bitcast.308, f32[2,128,8,2,64]{4,1,3,2,0:T(8,128)} %bitcast.307), kind=kLoop, calls=%fused_computation.9 | loop fusion | flops 1572864 | bytes 3145728 | tf_op jit(solution)/shard_map/convert_element_type | solution.py:132
  24.2 2.1 broadcast_select_fusion
  26.2 1.9 collective-permute-start
  28.2 2.4 fusion.15
  30.6 7.0 %collective-permute-start.3 = (bf16[2,128,1024]{1,2,0:T(8,128)(2,1)}, bf16[2,128,1024]{1,2,0:T(8,128)(2,1)}, u32[]{:S(2)}, u32[]{:S(2)}) collective-permute-start(bf16[2,128,1024]{1,2,0:T(8,128)(2,1)} %get-tuple-element.50), channel_id=1, source_target_pairs={{1,0},{2,1},{3,2},{4,3},{5,4},{6,5},{7,6},{8,7},{9,8},{10,9},{11,1... | collective-permute-start | bytes 1572872 | tf_op jit(solution)/shard_map/ppermute | solution.py:23
  38.4 2.6 reshape.655
  40.9 3.7 %copy.247 = bf16[2,128,8,2,128]{1,4,3,2,0:T(8,128)(2,1)} copy(bf16[2,128,8,2,128]{4,3,2,1,0:T(2,128)(2,1)} %reshape.655) | data formatting | bytes 2097152 | tf_op jit(solution)/shard_map/reshape | solution.py:139
  44.6 2.2 collective-permute-start.2
  50.8 8.0 %collective-permute-done.2 = bf16[2,128,1024]{1,2,0:T(8,128)(2,1)S(1)} collective-permute-done((bf16[2,128,1024]{1,2,0:T(8,128)(2,1)}, bf16[2,128,1024]{1,2,0:T(8,128)(2,1)S(1)}, u32[]{:S(2)}, u32[]{:S(2)}) %collective-permute-start.2) | collective-permute-done | bytes 524320 | tf_op jit(solution)/shard_map/ppermute | solution.py:23
  62.0 2.4 bitcast_convert_fusion
  64.3 4.2 %copy.285 = f32[2,8,2,128,128]{4,2,1,3,0:T(2,128)} copy(f32[2,8,2,128,128]{3,4,2,1,0:T(8,128)} %get-tuple-element.92) | data formatting | bytes 4194304
  68.5 5.1 %multiply_reduce_fusion = f32[2,8,2,128]{2,1,3,0:T(8,128)} fusion(f32[2,8,2,128,128]{4,2,1,3,0:T(2,128)} %copy.285, bf16[2,128,8,2,128]{4,3,2,1,0:T(2,128)(2,1)} %reshape.655), kind=kLoop, calls=%fused_computation.40 | loop fusion | flops 1568768 | bytes 3162112
  73.6 2.2 copy.286
  75.8 2.5 fusion.49
  83.5 2.1 collective-permute-start.5
  88.5 9.3 %collective-permute-done.5 = f32[2,128,1024]{1,2,0:T(8,128)S(1)} collective-permute-done((f32[2,128,1024]{1,2,0:T(8,128)S(1)}, f32[2,128,1024]{1,2,0:T(8,128)S(1)}, u32[]{:S(2)}, u32[]{:S(2)}) %collective-permute-start.5) | collective-permute-done | bytes 1048608 | tf_op jit(solution)/shard_map/ppermute | solution.py:23
  99.3 1.9 collective-permute-start.4
  101.2 7.4 %collective-permute-start.6 = (f32[2,128,1024]{1,2,0:T(8,128)}, f32[2,128,1024]{1,2,0:T(8,128)}, u32[]{:S(2)}, u32[]{:S(2)}) collective-permute-start(f32[2,128,1024]{1,2,0:T(8,128)} %get-tuple-element.46), channel_id=1, source_target_pairs={{1,0},{2,1},{3,2},{4,3},{5,4},{6,5},{7,6},{8,7},{9,8},{10,9},{11,1... | collective-permute-start | bytes 3145736 | tf_op jit(solution)/shard_map/ppermute | solution.py:23
  110.1 3.3 %copy.325 = f32[2,128,16,64]{3,2,1,0:T(8,128)} copy(f32[2,128,16,64]{1,3,2,0:T(8,128)} %get-tuple-element.60) | data formatting | bytes 2097152
  113.4 3.3 %copy.326 = f32[2,128,16,64]{3,2,1,0:T(8,128)} copy(f32[2,128,16,64]{1,3,2,0:T(8,128)} %get-tuple-element.61) | data formatting | bytes 2097152
  116.7 1.9 fusion.89
  121.0 3.0 %fusion.32 = (f32[1,2,128,1024]{2,3,1,0:T(8,128)S(1)}, f32[2,128,1024]{1,2,0:T(8,128)}) fusion(f32[2,1,128,1024]{2,3,1,0:T(8,128)S(1)} %bitcast.301, f32[2,1,128,1024]{2,3,1,0:T(8,128)S(1)} %bitcast.319, f32[2,128,1024]{1,2,0:T(8,128)} %collective-permute-done.6, pred[]{:T(512)S(6)} %eq.6, f32[2,1,128,1024]{2,3,1,0:T(8,128)S(1)} %bitcast.323, ...), kind=kLoop, calls=%fused_computation.63 | loop fusion | flops 1572864 | bytes 8388610 | tf_op jit(solution)/shard_map/stack | solution.py:199
  124.0 2.0 collective-permute-start.7
  126.7 2.5 multiply_reduce_fusion.1
  133.6 4.8 %fusion = bf16[2,128,16,128]{3,2,1,0:T(8,128)(2,1)} fusion(f32[2,128,16]{2,1,0:T(8,128)} %copy.243, f32[128]{0:T(128)} %param.11, f32[2,128,16]{2,1,0:T(8,128)S(1)} %copy.218, f32[2,128,16,64]{3,2,1,0:T(8,128)} %copy-done.1, f32[2,128,16,64]{3,2,1,0:T(8,128)} %copy-done, f32[2,128,16,128]{3,2,1,0:T(8,128)S(1)} %bitcast.300), kind=kLoop, calls=%fused_computation.1 | loop fusion | flops 3670016 | bytes 5276160 | tf_op jit(solution)/shard_map/convert_element_type | solution.py:207
  138.5 2.4 convert_element_type.84
  142.2 1.9 collective-permute-done.7
  154.3 10.5 %all-reduce.5 = (f32[128]{0:T(128)S(1)}, f32[128]{0:T(128)S(1)}) all-reduce(f32[128]{0:T(128)S(1)} %copy-done.72, f32[128]{0:T(128)S(1)} %get-tuple-element.38), channel_id=1, replica_groups=mesh['dp'=4,'ctx'=64] {'dp'}, use_global_device_ids=true, to_apply=%region_8.9 | all-reduce | flops 256 | bytes 2048 | tf_op jit(solution)/shard_map/psum | solution.py:15
  164.7 125.9 %all-reduce.4 = (f32[128]{0:T(128)}, f32[128]{0:T(128)}) all-reduce(f32[128]{0:T(128)S(1)} %get-tuple-element.42, f32[128]{0:T(128)S(1)} %get-tuple-element.43), channel_id=1, replica_groups=mesh['dp'=4,'ctx'=64] {'ctx'}, use_global_device_ids=true, to_apply=%region_9.10 | all-reduce | flops 256 | bytes 2048 | tf_op jit(solution)/shard_map/psum | solution.py:16
  (217 shorter events, 49.8 us)
Async XLA Ops:
  0.6 4.7 %copy-start.61 = (f32[128]{0:T(128)S(1)}, f32[128]{0:T(128)}, u32[]{:S(2)}) copy-start(f32[128]{0:T(128)} %param.12) | copy-start | bytes 1540
  6.5 5.8 %copy-start.8 = (bf16[2,128,8,128]{3,1,2,0:T(8,128)(2,1)}, bf16[2,128,8,128]{3,1,2,0:T(8,128)(2,1)S(1)}, u32[]{:S(2)}) copy-start(bf16[2,128,8,128]{3,1,2,0:T(8,128)(2,1)S(1)} %maximum_convert_fusion) | copy-start | bytes 1572868
  7.2 5.1 %copy-start.19 = (bf16[2,128,8,128]{1,3,2,0:T(8,128)(2,1)}, bf16[2,128,8,128]{1,3,2,0:T(8,128)(2,1)S(1)}, u32[]{:S(2)}) copy-start(bf16[2,128,8,128]{1,3,2,0:T(8,128)(2,1)S(1)} %copy.223) | copy-start | bytes 1572868
  7.5 4.8 %copy-start.21 = (bf16[2,128,1024]{1,2,0:T(8,128)(2,1)}, bf16[2,128,1024]{1,2,0:T(8,128)(2,1)S(1)}, u32[]{:S(2)}) copy-start(bf16[2,128,1024]{1,2,0:T(8,128)(2,1)S(1)} %copy.224) | copy-start | bytes 1572868
  8.4 15.8 %collective-permute-start.1 = (bf16[2,128,1024]{1,2,0:T(8,128)(2,1)}, bf16[2,128,1024]{1,2,0:T(8,128)(2,1)}, u32[]{:S(2)}, u32[]{:S(2)}) collective-permute-start(bf16[2,128,1024]{1,2,0:T(8,128)(2,1)} %fusion.65), channel_id=1, source_target_pairs={{1,0},{2,1},{3,2},{4,3},{5,4},{6,5},{7,6},{8,7},{9,8},{10,9},{11,1... | collective-permute-start | bytes 1572872 | tf_op jit(solution)/shard_map/ppermute | solution.py:23
  20.1 3.1 %copy-start.63 = (pred[2]{0:T(512)(128)(4,1)S(1)}, pred[2]{0:T(512)(128)(4,1)}, u32[]{:S(2)}) copy-start(pred[2]{0:T(512)(128)(4,1)} %get-tuple-element.80) | copy-start | bytes 10
  20.1 3.1 %copy-start.64 = (pred[2]{0:T(512)(128)(4,1)S(1)}, pred[2]{0:T(512)(128)(4,1)}, u32[]{:S(2)}) copy-start(pred[2]{0:T(512)(128)(4,1)} %get-tuple-element.81) | copy-start | bytes 10
  20.1 3.1 %copy-start.65 = (pred[2]{0:T(512)(128)(4,1)S(1)}, pred[2]{0:T(512)(128)(4,1)}, u32[]{:S(2)}) copy-start(pred[2]{0:T(512)(128)(4,1)} %get-tuple-element.82) | copy-start | bytes 10
  20.1 3.1 %copy-start.66 = (pred[2]{0:T(512)(128)(4,1)S(1)}, pred[2]{0:T(512)(128)(4,1)}, u32[]{:S(2)}) copy-start(pred[2]{0:T(512)(128)(4,1)} %get-tuple-element.83) | copy-start | bytes 10
  20.2 3.1 %copy-start.58 = (s32[2,128]{1,0:T(2,128)S(1)}, s32[2,128]{1,0:T(2,128)}, u32[]{:S(2)}) copy-start(s32[2,128]{1,0:T(2,128)} %get-tuple-element.53) | copy-start | bytes 3076
  20.2 3.1 %copy-start.71 = (s32[2,128]{1,0:T(2,128)S(1)}, s32[2,128]{1,0:T(2,128)}, u32[]{:S(2)}) copy-start(s32[2,128]{1,0:T(2,128)} %param.10) | copy-start | bytes 3076
  20.2 3.9 %copy-start.20 = (bf16[2,128,8,128]{1,3,2,0:T(8,128)(2,1)S(1)}, bf16[2,128,8,128]{1,3,2,0:T(8,128)(2,1)}, u32[]{:S(2)}) copy-start(bf16[2,128,8,128]{1,3,2,0:T(8,128)(2,1)} %copy-done.19) | copy-start | bytes 1572868
  20.2 3.9 %copy-start.22 = (bf16[2,128,1024]{1,2,0:T(8,128)(2,1)S(1)}, bf16[2,128,1024]{1,2,0:T(8,128)(2,1)}, u32[]{:S(2)}) copy-start(bf16[2,128,1024]{1,2,0:T(8,128)(2,1)} %copy-done.21) | copy-start | bytes 1572868
  23.2 5.0 %copy-start.9 = (bf16[2,128,8,128]{3,1,2,0:T(8,128)(2,1)S(1)}, bf16[2,128,8,128]{3,1,2,0:T(8,128)(2,1)}, u32[]{:S(2)}) copy-start(bf16[2,128,8,128]{3,1,2,0:T(8,128)(2,1)} %copy-done.8) | copy-start | bytes 1572868
  24.1 6.5 %copy-start.49 = (pred[2,128,128]{1,2,0:T(8,128)(4,1)}, pred[2,128,128]{1,2,0:T(8,128)(4,1)S(1)}, u32[]{:S(2)}) copy-start(pred[2,128,128]{1,2,0:T(8,128)(4,1)S(1)} %get-tuple-element.70) | copy-start | bytes 98308
  26.2 18.4 %collective-permute-start = (bf16[2,128,1024]{1,2,0:T(8,128)(2,1)}, bf16[2,128,1024]{1,2,0:T(8,128)(2,1)}, u32[]{:S(2)}, u32[]{:S(2)}) collective-permute-start(bf16[2,128,1024]{1,2,0:T(8,128)(2,1)} %get-tuple-element.51), channel_id=1, source_target_pairs={{0,1},{1,2},{2,3},{3,4},{4,5},{5,6},{6,7},{7,8},{8,9},{9,10},{10,1... | collective-permute-start | bytes 1572872 | tf_op jit(solution)/shard_map/ppermute | solution.py:23
  30.6 18.2 %collective-permute-start.3 = (bf16[2,128,1024]{1,2,0:T(8,128)(2,1)}, bf16[2,128,1024]{1,2,0:T(8,128)(2,1)}, u32[]{:S(2)}, u32[]{:S(2)}) collective-permute-start(bf16[2,128,1024]{1,2,0:T(8,128)(2,1)} %get-tuple-element.50), channel_id=1, source_target_pairs={{1,0},{2,1},{3,2},{4,3},{5,4},{6,5},{7,6},{8,7},{9,8},{10,9},{11,1... | collective-permute-start | bytes 1572872 | tf_op jit(solution)/shard_map/ppermute | solution.py:23
  44.6 3.5 %copy-start.43 = (pred[2,128,128]{1,2,0:T(8,128)(4,1)S(1)}, pred[2,128,128]{1,2,0:T(8,128)(4,1)}, u32[]{:S(2)}) copy-start(pred[2,128,128]{1,2,0:T(8,128)(4,1)} %get-tuple-element.72) | copy-start | bytes 98308
  44.6 14.2 %collective-permute-start.2 = (bf16[2,128,1024]{1,2,0:T(8,128)(2,1)}, bf16[2,128,1024]{1,2,0:T(8,128)(2,1)S(1)}, u32[]{:S(2)}, u32[]{:S(2)}) collective-permute-start(bf16[2,128,1024]{1,2,0:T(8,128)(2,1)} %collective-permute-done), channel_id=1, source_target_pairs={{0,1},{1,2},{2,3},{3,4},{4,5},{5,6},{6,7},{7,8},{8,9},{9,10},{10,1... | collective-permute-start | bytes 1572872 | tf_op jit(solution)/shard_map/ppermute | solution.py:23
  50.8 8.1 %copy-start.45 = (pred[2,128,128]{1,2,0:T(8,128)(4,1)S(1)}, pred[2,128,128]{1,2,0:T(8,128)(4,1)}, u32[]{:S(2)}) copy-start(pred[2,128,128]{1,2,0:T(8,128)(4,1)} %get-tuple-element.71) | copy-start | bytes 98308
  60.9 3.5 %copy-start.56 = (f32[2,2,8,128]{3,2,1,0:T(8,128)}, f32[2,2,8,128]{3,2,1,0:T(8,128)S(1)}, u32[]{:S(2)}) copy-start(f32[2,2,8,128]{3,2,1,0:T(8,128)S(1)} %add_add_fusion.2) | copy-start | bytes 49156
  82.9 3.1 %copy-start.26 = (bf16[2,8,2,128,128]{3,4,2,1,0:T(8,128)(2,1)}, bf16[2,8,2,128,128]{3,4,2,1,0:T(8,128)(2,1)S(1)}, u32[]{:S(2)}) copy-start(bf16[2,8,2,128,128]{3,4,2,1,0:T(8,128)(2,1)S(1)} %fusion.5) | copy-start | bytes 3145732
  83.5 14.4 %collective-permute-start.5 = (f32[2,128,1024]{1,2,0:T(8,128)S(1)}, f32[2,128,1024]{1,2,0:T(8,128)S(1)}, u32[]{:S(2)}, u32[]{:S(2)}) collective-permute-start(f32[2,128,1024]{1,2,0:T(8,128)S(1)} %fusion.44), channel_id=1, source_target_pairs={{1,0},{2,1},{3,2},{4,3},{5,4},{6,5},{7,6},{8,7},{9,8},{10,9},{11,1... | collective-permute-start | bytes 3145736 | tf_op jit(solution)/shard_map/ppermute | solution.py:23
  87.5 10.3 %copy-start.6 = (f32[2,8,128,128,1]{3,2,4,1,0:T(8,128)}, f32[2,8,128,128,1]{3,2,4,1,0:T(8,128)S(1)}, u32[]{:S(2)}) copy-start(f32[2,8,128,128,1]{3,2,4,1,0:T(8,128)S(1)} %fusion.88) | copy-start | bytes 3145732
  88.5 10.8 %copy-start.27 = (f32[2,8,128,128,1]{2,3,4,1,0:T(8,128)}, f32[2,8,128,128,1]{2,3,4,1,0:T(8,128)S(1)}, u32[]{:S(2)}) copy-start(f32[2,8,128,128,1]{2,3,4,1,0:T(8,128)S(1)} %fusion.47) | copy-start | bytes 3145732
  99.3 21.1 %collective-permute-start.4 = (f32[2,128,1024]{1,2,0:T(8,128)}, f32[2,128,1024]{1,2,0:T(8,128)}, u32[]{:S(2)}, u32[]{:S(2)}) collective-permute-start(f32[2,128,1024]{1,2,0:T(8,128)} %get-tuple-element.47), channel_id=1, source_target_pairs={{0,1},{1,2},{2,3},{3,4},{4,5},{5,6},{6,7},{7,8},{8,9},{9,10},{10,1... | collective-permute-start | bytes 3145736 | tf_op jit(solution)/shard_map/ppermute | solution.py:23
  101.2 19.8 %collective-permute-start.6 = (f32[2,128,1024]{1,2,0:T(8,128)}, f32[2,128,1024]{1,2,0:T(8,128)}, u32[]{:S(2)}, u32[]{:S(2)}) collective-permute-start(f32[2,128,1024]{1,2,0:T(8,128)} %get-tuple-element.46), channel_id=1, source_target_pairs={{1,0},{2,1},{3,2},{4,3},{5,4},{6,5},{7,6},{8,7},{9,8},{10,9},{11,1... | collective-permute-start | bytes 3145736 | tf_op jit(solution)/shard_map/ppermute | solution.py:23
  120.3 3.7 %copy-start.25 = (f32[2,8,128,128,1]{2,3,4,1,0:T(8,128)}, f32[2,8,128,128,1]{2,3,4,1,0:T(8,128)S(1)}, u32[]{:S(2)}) copy-start(f32[2,8,128,128,1]{2,3,4,1,0:T(8,128)S(1)} %fusion.45) | copy-start | bytes 3145732
  121.0 5.1 %copy-start.15 = (f32[2,128,16,64]{3,2,1,0:T(8,128)S(1)}, f32[2,128,16,64]{3,2,1,0:T(8,128)}, u32[]{:S(2)}) copy-start(f32[2,128,16,64]{3,2,1,0:T(8,128)} %copy.325) | copy-start | bytes 3145732
  121.0 5.1 %copy-start.16 = (f32[2,128,16,64]{3,2,1,0:T(8,128)S(1)}, f32[2,128,16,64]{3,2,1,0:T(8,128)}, u32[]{:S(2)}) copy-start(f32[2,128,16,64]{3,2,1,0:T(8,128)} %copy.326) | copy-start | bytes 3145732
  124.0 20.1 %collective-permute-start.7 = (f32[2,128,1024]{1,2,0:T(8,128)}, f32[2,128,1024]{1,2,0:T(8,128)}, u32[]{:S(2)}, u32[]{:S(2)}) collective-permute-start(f32[2,128,1024]{1,2,0:T(8,128)} %get-tuple-element.45), channel_id=1, source_target_pairs={{0,1},{1,2},{2,3},{3,4},{4,5},{5,6},{6,7},{7,8},{8,9},{9,10},{10,1... | collective-permute-start | bytes 3145736 | tf_op jit(solution)/shard_map/ppermute | solution.py:23
  138.5 5.6 %copy-start.5 = (f32[2,8,128,128,1]{3,2,4,1,0:T(8,128)S(1)}, f32[2,8,128,128,1]{3,2,4,1,0:T(8,128)}, u32[]{:S(2)}) copy-start(f32[2,8,128,128,1]{3,2,4,1,0:T(8,128)} %copy-done.4) | copy-start | bytes 3145732
  (49 other events, 102.3 us)
